TPU v7x, 32 devices: a whole 2x2x4 slice. The times are simulated.
32 devices in a mesh: dp: 8 (over y, x, core), tensor: 4 (over z).
Axes of the slice: x: 2, y: 2, z: 4, core: 2. Of those that a mesh axis runs over, the one named last changes fastest.
Arguments:
- tokens: bfloat16 [16384, 1024], P(('dp', 'tensor')), may hold values from -6 to 6
- cotangent: bfloat16 [16384, 1024], P(('dp', 'tensor')), may hold values from -6 to 6
- lengths: int32 [32], replicated, may hold values from 1 to 1024, as said below
- deal: int32 [32], replicated, may hold values from 0 to 31, as said below
- w_qkv: bfloat16 [3, 1024, 1024], P(None, 'dp', 'tensor'), may hold values from -0.1875 to 0.1875
- w_o: bfloat16 [1024, 1024], P('tensor', 'dp'), may hold values from -0.1875 to 0.1875
- w_1: bfloat16 [1024, 4096], P('dp', 'tensor'), may hold values from -0.1875 to 0.1875
- w_2: bfloat16 [4096, 1024], P('tensor', 'dp'), may hold values from -0.09375 to 0.09375
- b_qv: float32 [2, 1024], P(None, 'tensor'), may hold values from -1.8 to 1.8
- b_o: float32 [1024], replicated, may hold values from -0.3 to 0.3
- b_1: float32 [4096], P('tensor'), may hold values from -1.8 to 1.8
- b_2: float32 [1024], replicated, may hold values from -1.2 to 1.2
- ln_gain: float32 [4, 1024], replicated, may hold values from 0.25 to 1.75
- ln_bias: float32 [4, 1024], replicated, may hold values from -1.8 to 1.8
Outputs:
- output: bfloat16 [16384, 1024], P(('dp', 'tensor'))
- input_grad: bfloat16 [16384, 1024], P(('dp', 'tensor'))
- w_qkv_grad: float32 [3, 1024, 1024], P(None, 'dp', 'tensor')
- w_o_grad: float32 [1024, 1024], P('tensor', 'dp')
- w_1_grad: float32 [1024, 4096], P('dp', 'tensor')
- w_2_grad: float32 [4096, 1024], P('tensor', 'dp')
- b_qv_grad: float32 [2, 1024], P(None, 'tensor')
- b_o_grad: float32 [1024], replicated
- b_1_grad: float32 [4096], P('tensor')
- b_2_grad: float32 [1024], replicated
- ln_gain_grad: float32 [4, 1024], replicated
- ln_bias_grad: float32 [4, 1024], replicated
Inputs may be any that keep to these rules, and one draw needn't show every extreme that they name: The 4 sequences that deal gives to one data group have lengths that sum to 2048, and one of them has exactly 1024 tokens. `deal`: A permutation of the sequences; slots b * 4 to b * 4 + 3 belong to data group b.
All inputs are finite; a program needn't handle non-finite values. Where the computation divides by a largest or mean magnitude, that divisor is 1e-20 or more.
Results may differ from a plain program's by a relative error of at most 0.015.
Values may be sent and summed in bfloat16 or wider, within the bound.
A program may use at most 192 MiB of HBM per device.

v0:
```python
from functools import partial

import jax
import jax.numpy as jnp
from jax import lax
from jax.experimental import pallas as pl
from jax.experimental.pallas import tpu as pltpu
from jax.sharding import PartitionSpec as P

DH = 64
HALF = 1024
NORM_EPS = 1e-05
MASKED_OUT = -1e30
BF, F32 = jnp.bfloat16, jnp.float32
QB = 256


def scaled_norm(values, norm_gain, norm_shift):
    peak = jnp.max(jnp.abs(values), axis=-1, keepdims=True) + NORM_EPS
    scaled = values / peak
    centred = scaled - jnp.mean(scaled, axis=-1, keepdims=True)
    spread = jnp.mean(centred * centred, axis=-1, keepdims=True)
    return centred * lax.rsqrt(spread + NORM_EPS) * norm_gain + norm_shift


def norm_back(values, norm_gain, norm_shift, row_grad):
    result, pull = jax.vjp(scaled_norm, values, norm_gain, norm_shift)
    return pull(row_grad)


PAIR = 2 * DH


def attn_fwd_kernel(qpos_ref, qstart_ref, kpos_ref, qkv_ref, o_ref, lse_ref):
    first = pl.multiple_of(pl.program_id(0) * QB, QB)
    kpos = kpos_ref[...]
    allowed = (kpos <= qpos_ref[...]) & (kpos >= qstart_ref[...])
    bias = jnp.where(allowed, 0.0, MASKED_OUT)
    lane = lax.broadcasted_iota(jnp.int32, (1, PAIR), 1)
    wide = lax.broadcasted_iota(jnp.int32, lse_ref.shape, 1)
    stats = jnp.zeros(lse_ref.shape, F32)
    for pair in range(o_ref.shape[1] // PAIR):
        at = 3 * pair * PAIR
        query = qkv_ref[pl.ds(first, QB), at:at + PAIR]
        key, value = qkv_ref[:, at + PAIR:at + 2 * PAIR], qkv_ref[:, at + 2 * PAIR:at + 3 * PAIR]
        total = jnp.zeros(query.shape, F32)
        for side in range(2):
            mine = (lane >= side * DH) & (lane < (side + 1) * DH)
            part = jnp.where(mine, query * 0.125, 0.0).astype(BF)
            score = lax.dot_general(part, key, (((1,), (1,)), ((), ())), preferred_element_type=F32) + bias
            peak = jnp.max(score, axis=-1, keepdims=True)
            expo = jnp.exp(score - peak)
            norm = jnp.sum(expo, axis=-1, keepdims=True)
            prob = (expo * (1.0 / norm)).astype(BF)
            total += jnp.dot(prob, jnp.where(mine, value, jnp.zeros_like(value)), preferred_element_type=F32)
            stats = jnp.where(wide == pair * 2 + side, peak + jnp.log(norm), stats)
        o_ref[:, pair * PAIR:(pair + 1) * PAIR] = total.astype(BF)
    lse_ref[...] = stats


def attn_forward(qpos, qstart, kpos, qkv):
    rows, width = qkv.shape[0], qkv.shape[1] // 3
    col = pl.BlockSpec((QB, 1), lambda i: (i, 0))
    full = pl.BlockSpec(qkv.shape, lambda i: (0, 0))
    return pl.pallas_call(
        attn_fwd_kernel,
        grid=(rows // QB,),
        in_specs=[col, col, pl.BlockSpec((1, rows), lambda i: (0, 0)), full],
        out_specs=[pl.BlockSpec((QB, width), lambda i: (i, 0)), pl.BlockSpec((QB, 128), lambda i: (i, 0))],
        out_shape=[jax.ShapeDtypeStruct((rows, width), BF), jax.ShapeDtypeStruct((rows, 128), F32)],
        cost_estimate=pl.CostEstimate(flops=4 * rows * rows * width, bytes_accessed=8 * rows * width, transcendentals=rows * rows * width // DH),
        compiler_params=pltpu.CompilerParams(vmem_limit_bytes=48 << 20),
        name="attn_fwd",
    )(qpos, qstart, kpos, qkv)


def attn_bwd_kernel(qpos_ref, qstart_ref, kpos_ref, lse_ref, g_ref, qkv_ref, d_ref, dk_acc, dv_acc):
    step = pl.program_id(0)
    first = pl.multiple_of(step * QB, QB)

    @pl.when(step == 0)
    def _():
        dk_acc[...] = jnp.zeros_like(dk_acc)
        dv_acc[...] = jnp.zeros_like(dv_acc)

    kpos = kpos_ref[...]
    allowed = (kpos <= qpos_ref[...]) & (kpos >= qstart_ref[...])
    bias = jnp.where(allowed, 0.0, MASKED_OUT)
    lane = lax.broadcasted_iota(jnp.int32, (1, PAIR), 1)
    for pair in range(g_ref.shape[1] // PAIR):
        at = 3 * pair * PAIR
        query = qkv_ref[pl.ds(first, QB), at:at + PAIR]
        key, value = qkv_ref[:, at + PAIR:at + 2 * PAIR], qkv_ref[:, at + 2 * PAIR:at + 3 * PAIR]
        cols = slice(pair * PAIR, (pair + 1) * PAIR)
        grad = g_ref[:, cols]
        dq = jnp.zeros(query.shape, F32)
        dk = jnp.zeros(key.shape, F32)
        dv = jnp.zeros(key.shape, F32)
        for side in range(2):
            mine = (lane >= side * DH) & (lane < (side + 1) * DH)
            part = jnp.where(mine, query * 0.125, 0.0).astype(BF)
            gpart = jnp.where(mine, grad, jnp.zeros_like(grad))
            score = lax.dot_general(part, key, (((1,), (1,)), ((), ())), preferred_element_type=F32) + bias
            index = pair * 2 + side
            prob = jnp.exp(score - lse_ref[:, index:index + 1])
            gprob = lax.dot_general(gpart, value, (((1,), (1,)), ((), ())), preferred_element_type=F32)
            inner = jnp.sum(prob * gprob, axis=-1, keepdims=True)
            gscore = (prob * (gprob - inner)).astype(BF)
            dq += jnp.dot(gscore, jnp.where(mine, key, jnp.zeros_like(key)), preferred_element_type=F32)
            dk += lax.dot_general(gscore, part, (((0,), (0,)), ((), ())), preferred_element_type=F32)
            dv += lax.dot_general(prob.astype(BF), gpart, (((0,), (0,)), ((), ())), preferred_element_type=F32)
        d_ref[pl.ds(first, QB), at:at + PAIR] = (dq * 0.125).astype(BF)
        dk_acc[:, cols] += dk
        dv_acc[:, cols] += dv

    @pl.when(step == pl.num_programs(0) - 1)
    def _():
        for pair in range(g_ref.shape[1] // PAIR):
            at = 3 * pair * PAIR
            cols = slice(pair * PAIR, (pair + 1) * PAIR)
            d_ref[:, at + PAIR:at + 2 * PAIR] = dk_acc[:, cols].astype(BF)
            d_ref[:, at + 2 * PAIR:at + 3 * PAIR] = dv_acc[:, cols].astype(BF)


def attn_backward(qpos, qstart, kpos, lse, grad, qkv):
    rows, width = grad.shape
    col = pl.BlockSpec((QB, 1), lambda i: (i, 0))
    full = pl.BlockSpec(qkv.shape, lambda i: (0, 0))
    return pl.pallas_call(
        attn_bwd_kernel,
        grid=(rows // QB,),
        in_specs=[col, col, pl.BlockSpec((1, rows), lambda i: (0, 0)), pl.BlockSpec((QB, 128), lambda i: (i, 0)),
                  pl.BlockSpec((QB, width), lambda i: (i, 0)), full],
        out_specs=full,
        out_shape=jax.ShapeDtypeStruct(qkv.shape, BF),
        scratch_shapes=[pltpu.VMEM((rows, width), F32), pltpu.VMEM((rows, width), F32)],
        cost_estimate=pl.CostEstimate(flops=10 * rows * rows * width, bytes_accessed=14 * rows * width, transcendentals=rows * rows * width // DH),
        compiler_params=pltpu.CompilerParams(vmem_limit_bytes=48 << 20),
        name="attn_bwd",
    )(qpos, qstart, kpos, lse, grad, qkv)


def swap_dp(x, bit):
    n = lax.axis_size("dp")
    return lax.ppermute(x, "dp", [(i, i ^ bit) for i in range(n)])


def turn(x, shift):
    n = lax.axis_size("tensor")
    return lax.ppermute(x, "tensor", [(i, (i + shift) % n) for i in range(n)])


def chip_bits():
    n = lax.axis_size("dp")
    return [1 << b for b in range(1, n.bit_length() - 1)]


def core_pair(mine, other):
    core = lax.axis_index("dp") % 2
    return jnp.where(core == 0, jnp.stack([mine, other]), jnp.stack([other, mine]))


def gather_weights(mine, other):
    pair = core_pair(mine, swap_dp(other, 1)).reshape(2 * mine.shape[0], mine.shape[1])
    lanes = lax.axis_size("tensor")
    column = jnp.stack([pair] + [turn(pair, k) for k in range(1, lanes)])
    bits = chip_bits()
    if len(bits) == 2:
        low, high = bits
        first, second = swap_dp(column, low), swap_dp(column, high)
        mid = lanes // 2
        far = jnp.concatenate([swap_dp(first[:mid], high), swap_dp(second[mid:], low)])
        return {0: column, low: first, high: second, low | high: far}
    blocks = {0: column}
    for bit in bits:
        got = swap_dp(jnp.stack([blocks[m] for m in sorted(blocks)]), bit)
        blocks.update({m | bit: got[i] for i, m in enumerate(sorted(blocks))})
    return blocks


def weight_of(blocks, start, width):
    out = []
    for mask in sorted(blocks):
        part = blocks[mask][:, :, start:start + width]
        out.append(jnp.concatenate([part[k] for k in range(part.shape[0])], axis=1))
    return jnp.concatenate(out, axis=0)


def scatter_grads(parts):
    lanes = lax.axis_size("tensor")
    bits = chip_bits()
    count = 1 << len(bits)
    feats = parts[0].shape[0]
    per = feats // count

    def block(mask_index, k):
        cut = []
        for p in parts:
            w = p.shape[1] // lanes
            cut.append(p[mask_index * per:(mask_index + 1) * per, k * w:(k + 1) * w])
        return jnp.concatenate(cut, axis=1) if len(cut) > 1 else cut[0]

    def col(mask_index, ks):
        return jnp.stack([block(mask_index, k) for k in ks])

    if len(bits) == 2:
        low, high = bits
        mid = lanes // 2
        ka, kb = list(range(mid)), list(range(mid, lanes))
        sent_a = jnp.stack([col(1, ka), col(3, ka)]).astype(BF)
        sent_b = jnp.stack([col(2, kb), col(3, kb)]).astype(BF)
        got_a, got_b = swap_dp(sent_a, low), swap_dp(sent_b, high)
        pass_a = (col(2, ka) + got_a[1].astype(F32)).astype(BF)
        pass_b = (col(1, kb) + got_b[1].astype(F32)).astype(BF)
        end_a, end_b = swap_dp(pass_a, high), swap_dp(pass_b, low)
        keep_a = col(0, ka) + got_a[0].astype(F32) + end_a.astype(F32)
        keep_b = col(0, kb) + got_b[0].astype(F32) + end_b.astype(F32)
        total = [keep_a[i] for i in range(mid)] + [keep_b[i] for i in range(lanes - mid)]
    else:
        sums = {m: col(m, range(lanes)) for m in range(count)}
        for level in reversed(range(len(bits))):
            keys = [m for m in sorted(sums) if m >> level & 1]
            got = swap_dp(jnp.stack([sums[m] for m in keys]).astype(BF), bits[level])
            sums = {m ^ (1 << level): sums[m ^ (1 << level)] + got[i].astype(F32) for i, m in enumerate(keys)}
        total = [sums[0][k] for k in range(lanes)]
    own = total[0]
    for k in range(1, lanes):
        own = own + turn(total[k].astype(BF), -k).astype(F32)
    rows = own.shape[0] // 2
    core = lax.axis_index("dp") % 2
    mine = lax.dynamic_slice_in_dim(own, core * rows, rows, 0)
    other = lax.dynamic_slice_in_dim(own, (1 - core) * rows, rows, 0)
    return core_pair(mine, swap_dp(other.astype(BF), 1).astype(F32))


def deal_perms(n_dp):
    near, far = [], []
    for chip in range(n_dp // 2):
        for c in range(2):
            for j in range(4):
                source = (chip * 2 + c) * 4 + j
                near.append((source, (chip * 2 + j % 2) * 4 + 2 * c + j // 2))
                far.append((source, (chip * 2 + j % 2) * 4 + 2 * c + 1 - j // 2))
    return near, far


MESH = pl.DeviceIdType.MESH
LANES = 4
ANY = pl.BlockSpec(memory_space=pl.ANY)
IN_VMEM = pl.BlockSpec(memory_space=pltpu.VMEM)


def greet(dp, lane, n_dp):
    barrier = pltpu.get_barrier_semaphore()
    count = 0
    for d in range(1, n_dp):
        pl.semaphore_signal(barrier, inc=1, device_id=(dp ^ d, lane), device_id_type=MESH)
        count += 1
    for k in range(1, LANES):
        for c in range(2):
            pl.semaphore_signal(barrier, inc=1, device_id=(dp ^ c, lax.rem(lane + k, LANES)), device_id_type=MESH)
            count += 1
    return barrier, count


def send(src, dst, send_sem, recv_sem, device):
    return pltpu.make_async_remote_copy(src_ref=src, dst_ref=dst, send_sem=send_sem, recv_sem=recv_sem, device_id=device, device_id_type=MESH)


DEAL_CUTS = 4
SMEM = pl.BlockSpec(memory_space=pltpu.SMEM)


class Pack:
    def __init__(self, lengths, deal, dp, lane, rows):
        core = dp % 2
        per = lengths.shape[0] // 8
        first = ((dp // 2) * 2 + lane // 2) * per
        self.starts, end, self.cut = [], 0, 0
        for j in range(per):
            size = lengths[deal[first + j]]
            self.starts.append(end)
            self.cut = self.cut + jnp.where(size == HALF, end, 0)
            end = end + size
        self.half, self.offset, self.rows = lane % 2, core * rows, rows

    def slots(self, begin, count, axis):
        shape = (count, 1) if axis == 0 else (1, count)
        return (self.offset + begin + lax.broadcasted_iota(jnp.int32, shape, axis)) & (2 * self.rows - 1)

    def places(self, begin, count, axis):
        slot = self.slots(begin, count, axis)
        return slot + HALF * jnp.where(slot >= self.cut, self.half, 1 - self.half)

    def seen_from(self, places):
        out = jnp.zeros(places.shape, jnp.int32)
        for start in self.starts:
            out = jnp.maximum(out, jnp.where(places >= start, start, 0))
        return out

    def bias(self, begin, kpos):
        at = self.places(begin, QB, 0)
        return jnp.where((kpos <= at) & (kpos >= self.seen_from(at)), 0.0, MASKED_OUT)


def relative(vec, chip, sources):
    quarter = vec.shape[1] // 4
    for q in range(4):
        cols = pl.ds(pl.multiple_of((chip ^ q) * quarter, quarter), quarter)
        at = 0
        for src in sources:
            count = src.shape[0]
            vec[at:at + count, q * quarter:(q + 1) * quarter] = src[:, cols]
            at += count


def norm_parts(x):
    peak = jnp.max(jnp.abs(x), axis=-1, keepdims=True) + NORM_EPS
    u = x * (1.0 / peak)
    c = u - jnp.mean(u, axis=-1, keepdims=True)
    return c, lax.rsqrt(jnp.mean(c * c, axis=-1, keepdims=True) + NORM_EPS)


def norm_rows(x, gain, shift):
    c, r = norm_parts(x)
    return c * r * gain + shift


def dot_t(a, b):
    return lax.dot_general(a, b, (((1,), (1,)), ((), ())), preferred_element_type=F32)


class Sems:
    def __init__(self, ref):
        self.ref, self.used = ref, 0

    def take(self, count=1):
        self.used += count
        return self.used - count


FWD_SEMS = 320


def forward_kernel(widths, lengths, deal, w_qkv, w_o, w_1, w_2, b_qv, b_1, b_o, b_2, ln_gain, ln_bias, tok, cot, *rest):
    outs, rest = rest[:18], rest[18:]
    (wq_o, wo_o, w1_o, w2_o, h_o, xin_o, qkv_o, heads_o, lse_o, attn_o, first_o, xmid_o, act_o, dg_o, ffn_o, res_o, grd_o, small_o) = outs
    (wq, wo, w1, w2, moved, cand, h, xin, qkv, heads, lse, part, sbuf, rbuf, first, xmid, act, dg, stage, small_in, own, other, small, vec, sem_ref) = rest
    mats = (wq, wo, w1, w2)
    sems = Sems(sem_ref)
    dp, lane = lax.axis_index("dp"), lax.axis_index("tensor")
    n_dp = 8
    core, chip = dp % 2, dp // 2
    rows, d = tok.shape
    wd = own.shape[0]
    quarter = d // 4
    up = lax.rem(lane + 1, LANES)
    n_g = len(widths)
    mate = (dp ^ 1, lane)
    ends = []

    def local(src, dst):
        c = pltpu.make_async_copy(src, dst, sem_ref.at[sems.take()])
        return c

    def remote(src, dst, device):
        s, r = sems.take(), sems.take()
        c = send(src, dst, sem_ref.at[s], sem_ref.at[r], device)
        ends.append(c.wait_send)
        return c

    barrier, count = greet(dp, lane, n_dp)
    rows_of = lambda x: jnp.transpose(x.astype(F32)).astype(BF)
    for half, dst in ((core, own), (1 - core, other)):
        at = 0
        part_of = lambda w: pl.ds(pl.multiple_of(half * w, w), w)
        for t in range(3):
            dst[:, at:at + widths[1]] = w_qkv[t, :, part_of(widths[1])]
            at += widths[1]
        for src, w, turned in ((w_o, widths[1], True), (w_1, widths[2], False), (w_2, widths[3], True)):
            dst[:, at:at + w] = rows_of(src[part_of(w), :]) if turned else src[:, part_of(w)]
            at += w
    at = 0
    small[...] = jnp.zeros_like(small)
    for src, w in ((b_qv.at[0:1], widths[1]), (b_qv.at[1:2], widths[1]), (b_1, widths[2])):
        small[0:1, at:at + w] = src[:, pl.ds(pl.multiple_of(core * w, w), w)]
        at += w
    relative(vec, chip, (ln_gain, ln_bias, b_o, b_2))
    held = Pack(lengths, deal, dp, lane, rows)
    pl.semaphore_wait(barrier, count)
    block = rows // n_dp
    here = pl.ds(pl.multiple_of(dp * block, block), block)
    deals = []
    for i, src in enumerate((tok, cot)):
        stay = local(src.at[here], moved.at[i, here])
        copies = []
        for k in range(1, n_dp):
            there = pl.ds(pl.multiple_of((dp ^ k) * block, block), block)
            copies.append(remote(src.at[there], moved.at[i, here], (dp ^ k, lane)))
        deals.append((stay, copies))

    def deal_start(i):
        deals[i][0].start()
        for c in deals[i][1]:
            c.start()

    deal_start(0)
    feat = pl.ds(pl.multiple_of(core * wd, wd), wd)
    at, stays, pairs = 0, [], []
    for g, w in enumerate(widths):
        dst = mats[g].at[feat, 0:w]
        stays.append(local(own.at[:, at:at + w], dst))
        pairs.append(remote(other.at[:, at:at + w], dst, mate))
        stays[g].start()
        pairs[g].start()
        at += w
    n_s = small.shape[0]
    smalls = [remote(small, small_in.at[k], (dp, lax.rem(lane + k, LANES))) for k in range(1, LANES)]
    for c in smalls:
        c.start()
    small_in[0] = small[...]

    def area(g, q, k):
        w = widths[g]
        return mats[g].at[2 * wd * q:2 * wd * (q + 1), k * w:(k + 1) * w]

    turns = [[remote(area(g, 0, t), area(g, 0, t + 1), (dp, up)) for t in range(LANES - 1)] for g in range(n_g)]
    planes = [[[remote(area(g, 0, k), area(g, side, k), (dp ^ (2 * side), lane)) for side in (1, 2)] for k in range(LANES)] for g in range(n_g)]
    fars = []
    for g in range(n_g):
        fars.append([])
        for k in range(LANES):
            side, via = (1, 2) if k < LANES // 2 else (2, 1)
            fars[g].append(remote(area(g, side, k), area(g, 3, k), (dp ^ (2 * via), lane)))

    def plane(g, k):
        for c in planes[g][k]:
            c.start()

    def pair_in(g):
        stays[g].wait()
        pairs[g].wait_recv()
        turns[g][0].start()

    def turn_in(g, t):
        turns[g][t].wait_recv()
        if t < LANES - 2:
            turns[g][t + 1].start()

    def far_go(g, k):
        planes[g][k][0 if k < LANES // 2 else 1].wait_recv()
        fars[g][k].start()

    def all_in(g):
        for k in range(LANES):
            planes[g][k][1 if k < LANES // 2 else 0].wait_recv()
            fars[g][k].wait_recv()

    pack = lane // 2
    spot = chip * 2 + lane % 2
    to_near = (spot, core + 1)
    slot = jnp.where(lane // 2 == core, 1, 0)
    is_self = (lane == 3 * core) & (spot == dp)
    is_near = lane == pack + 1
    straight = core == pack
    split = jnp.where(jnp.logical_not(is_near) & jnp.logical_not(straight), 2 * HALF, held.cut)
    cut = rows // DEAL_CUTS

    class Route:
        def __init__(self, i):
            self.i = i
            a0, f0 = sems.take(DEAL_CUTS), sems.take(DEAL_CUTS)
            got = sems.take(2 * DEAL_CUTS)
            self.near, self.self_, self.hand, self.pick, self.wait0, self.wait1 = [], [], [], [], [], []
            for n in range(DEAL_CUTS):
                rs = slice(n * cut, (n + 1) * cut)
                src = moved.at[i, rs]
                last = (dp, 3 * pack)
                self.near.append(send(src, cand.at[i, slot, rs], sem_ref.at[a0 + n], sem_ref.at[got + n * 2 + slot], to_near))
                self.self_.append(pltpu.make_async_copy(src, cand.at[i, 0, rs], sem_ref.at[got + n * 2]))
                self.hand.append(send(cand.at[i, 0, rs], cand.at[i, 1, rs], sem_ref.at[f0 + n], sem_ref.at[got + n * 2 + 1], last))
                self.pick.append(send(stage.at[0, rs], cand.at[i, 1, rs], sem_ref.at[f0 + n], sem_ref.at[got + n * 2 + 1], last))
                self.wait0.append(send(src, cand.at[i, 0, rs], sem_ref.at[a0 + n], sem_ref.at[got + n * 2], to_near))
                self.wait1.append(send(src, cand.at[i, 1, rs], sem_ref.at[a0 + n], sem_ref.at[got + n * 2 + 1], to_near))

        def start(self):
            for n in range(DEAL_CUTS):
                self.near[n].start()
                pl.when(is_self)(lambda: self.self_[n].start())

        def arrive(self, n):
            pl.when(is_self)(lambda: self.self_[n].wait())
            pl.when(is_near)(lambda: self.wait0[n].wait_recv())
            pl.when(is_near & straight)(lambda: self.hand[n].start())
            self.wait1[n].wait_recv()

            def choose_far():
                rs = slice(n * cut, (n + 1) * cut)
                on = held.slots(n * cut, cut, 0) >= held.cut
                stage[0, rs] = jnp.where(on, cand[self.i, 1, rs].astype(F32), cand[self.i, 0, rs].astype(F32)).astype(BF)
                self.pick[n].start()

            pl.when(is_near & jnp.logical_not(straight))(choose_far)

        def finish(self, picked=True):
            for n in range(DEAL_CUTS):
                self.near[n].wait_send()
                pl.when(is_near & straight)(lambda: self.hand[n].wait_send())
                if picked:
                    pl.when(is_near & jnp.logical_not(straight))(lambda: self.pick[n].wait_send())

    routes = [Route(0), Route(1)]

    def deal_on(i):
        deals[i][0].wait()
        for c in deals[i][1]:
            c.wait_recv()
        routes[i].start()

    def choose(i, n):
        rs = slice(n * cut, (n + 1) * cut)
        on = held.slots(n * cut, cut, 0) >= split
        parts = []
        for q in range(4):
            cols = pl.ds(pl.multiple_of((chip ^ q) * quarter, quarter), quarter)
            parts.append(jnp.where(on, cand[i, 0, rs, cols].astype(F32), cand[i, 1, rs, cols].astype(F32)))
        return jnp.concatenate(parts, axis=1)

    out_copies = []

    def put(src, dst):
        c = local(src, dst)
        c.start()
        out_copies.append(c)

    early = (0, 1)

    def forward_on(groups, t):
        for g in groups:
            turn_in(g, t)
        for g in groups:
            plane(g, t + 1)

    for g in (0, 1, 2):
        pair_in(g)
        plane(g, 0)
    forward_on(early, 0)
    forward_on((2,), 0)
    forward_on(early, 1)
    deal_on(0)
    forward_on((2,), 1)
    forward_on(early, 2)
    for k in range(LANES):
        for g in early:
            far_go(g, k)
    pair_in(3)
    plane(3, 0)
    deal_start(1)
    joins = []

    def join_send(x, n, size):
        c = remote(x.at[n * size:(n + 1) * size], x.at[rows + n * size:rows + (n + 1) * size], mate)
        c.start()
        joins.append(c)

    gains = lambda i: vec[i:i + 1, :]
    for n in range(DEAL_CUTS):
        rs = slice(n * cut, (n + 1) * cut)
        routes[0].arrive(n)
        x = choose(0, n)
        h[rs, :] = x.astype(BF)
        xin[rs, :] = norm_rows(x, gains(0), gains(4)).astype(BF)
        join_send(xin, n, cut)
        if n == 2:
            forward_on((2,), 2)
    forward_on((3,), 0)
    for c in smalls:
        c.wait_recv()
    all_in(0)
    for c in joins:
        c.wait_recv()
    put(wq, wq_o)
    put(h, h_o)
    put(xin, xin_o)
    w = widths[0]
    third = w // 3
    for k in range(LANES):
        cols = slice(k * w, (k + 1) * w)
        row = small_in[k, 0:1, :]
        bias = jnp.concatenate([row[:, 0:third], jnp.zeros((1, third), F32), row[:, third:2 * third]], axis=1)

        def project(r, carry, cols=cols, bias=bias):
            rs = pl.ds(pl.multiple_of(r * QB, QB), QB)
            qkv[rs, cols] = (jnp.dot(xin[rs, :], wq[:, cols], preferred_element_type=F32) + bias).astype(BF)
            return carry

        lax.fori_loop(0, 2 * rows // QB, project, 0)
        far_go(2, k)
    put(qkv, qkv_o)
    forward_on((3,), 1)

    kpos = held.places(0, 2 * rows, 1)

    def beside(i):
        if i == 0:
            deal_on(1)
        elif i == 1:
            forward_on((3,), 2)
        elif i == 2:
            far_go(3, 0)
            far_go(3, 1)

    def attend(i, carry):
        begin = pl.multiple_of(i * QB, QB)
        attn_block(pl.ds(begin, QB), held.bias(begin, kpos), qkv, heads, lse)
        for n in range(3):
            pl.when(i == n)(lambda: beside(n))
        return carry

    lax.fori_loop(0, 2 * rows // QB, attend, 0)
    put(heads, heads_o)
    put(lse, lse_o)
    all_in(1)
    put(wo, wo_o)

    def fold(x, w_ref, which):
        copies = []
        per = 2
        size = rows // per
        for n in range(per):
            rs = slice(rows + n * size, rows + (n + 1) * size)
            sbuf[which, n * size:(n + 1) * size] = dot_t(x[rs, :], w_ref[...]).astype(BF)
            c = remote(sbuf.at[which, n * size:(n + 1) * size], rbuf.at[which, n * size:(n + 1) * size], mate)
            c.start()
            copies.append(c)
        for n in range(per):
            rs = slice(n * size, (n + 1) * size)
            part[rs, :] = dot_t(x[rs, :], w_ref[...])
        return copies

    copies = fold(heads, wo, 0)
    joins.clear()
    size = rows // 2
    for n in range(2):
        copies[n].wait_recv()

        def middle(m, carry, n=n):
            rs = pl.ds(pl.multiple_of(n * size + m * cut, cut), cut)
            y = part[rs, :] + rbuf[0, rs].astype(F32) + gains(8)
            part[rs, :] = y
            f = h[rs, :].astype(F32) + norm_rows(y, gains(1), gains(5))
            first[rs, :] = f
            xmid[rs, :] = norm_rows(f, gains(2), gains(6)).astype(BF)
            return carry

        lax.fori_loop(0, size // cut, middle, 0)
        join_send(xmid, n, size)
    attn_put = local(part, attn_o)
    attn_put.start()
    put(first, first_o)
    all_in(2)
    put(w1, w1_o)
    for c in joins:
        c.wait_recv()
    put(xmid, xmid_o)
    w = widths[2]
    for k in range(LANES):
        cols = slice(k * w, (k + 1) * w)
        bias = small_in[k, 0:1, 2 * third:2 * third + w]

        def hidden_units(r, carry, cols=cols, bias=bias):
            rs = pl.ds(pl.multiple_of(r * QB, QB), QB)
            pre = jnp.dot(xmid[rs, :], w1[:, cols], preferred_element_type=F32) + bias
            cdf = 0.5 + 0.5 * lax.erf(pre * 0.7071067811865476)
            act[rs, cols] = (pre * cdf).astype(BF)
            dg[rs, cols] = (cdf + pre * (0.3989422804014327 * jnp.exp(-0.5 * pre * pre))).astype(BF)
            return carry

        lax.fori_loop(0, 2 * rows // QB, hidden_units, 0)
        if k < 2:
            far_go(3, k + 2)
        if k == 1:
            routes[0].finish()
        if k > 1:
            routes[1].arrive(2 * k - 4)
            routes[1].arrive(2 * k - 3)
    put(act, act_o)
    put(dg, dg_o)
    all_in(3)
    put(w2, w2_o)
    attn_put.wait()
    copies = fold(act, w2, 1)
    for n in range(DEAL_CUTS):
        rs = slice(n * cut, (n + 1) * cut)
        stage[1, rs] = choose(1, n).astype(BF)
    put(stage.at[1], grd_o)
    for n in range(DEAL_CUTS):
        pl.when(is_near & jnp.logical_not(straight))(lambda: routes[1].pick[n].wait_send())
    for n in range(2):
        copies[n].wait_recv()

        def last(m, carry, n=n):
            rs = pl.ds(pl.multiple_of(n * size + m * cut, cut), cut)
            y = part[rs, :] + rbuf[1, rs].astype(F32) + gains(9)
            part[rs, :] = y
            out = first[rs, :] + norm_rows(y, gains(3), gains(7))
            for q in range(4):
                cols = pl.ds(pl.multiple_of((chip ^ q) * quarter, quarter), quarter)
                stage[0, rs, cols] = out[:, q * quarter:(q + 1) * quarter].astype(BF)
            return carry

        lax.fori_loop(0, size // cut, last, 0)
    put(part, ffn_o)
    put(stage.at[0], res_o)
    put(small_in, small_o)
    for c in out_copies:
        c.wait()
    routes[1].finish(False)
    for wait in ends:
        wait()


def attn_block(rs, bias, qkv, heads, lse):
    lane = lax.broadcasted_iota(jnp.int32, (1, PAIR), 1)
    wide = lax.broadcasted_iota(jnp.int32, (QB, 128), 1)
    stats = jnp.zeros((QB, 128), F32)
    for pair in range(heads.shape[1] // PAIR):
        at = 3 * pair * PAIR
        query = qkv[rs, at:at + PAIR]
        key, value = qkv[:, at + PAIR:at + 2 * PAIR], qkv[:, at + 2 * PAIR:at + 3 * PAIR]
        total = jnp.zeros(query.shape, F32)
        for side in range(2):
            mine = (lane >= side * DH) & (lane < (side + 1) * DH)
            piece = jnp.where(mine, query * 0.125, 0.0).astype(BF)
            score = dot_t(piece, key) + bias
            peak = jnp.max(score, axis=-1, keepdims=True)
            expo = jnp.exp(score - peak)
            norm = jnp.sum(expo, axis=-1, keepdims=True)
            prob = (expo * (1.0 / norm)).astype(BF)
            total += jnp.dot(prob, jnp.where(mine, value, jnp.zeros_like(value)), preferred_element_type=F32)
            stats = jnp.where(wide == pair * 2 + side, peak + jnp.log(norm), stats)
        heads[rs, pair * PAIR:(pair + 1) * PAIR] = total.astype(BF)
    lse[rs, :] = stats


def forward_call(widths, tok, cot, lengths, deal, w_qkv, w_o, w_1, w_2, b_qv, b_1, b_o, b_2, ln_gain, ln_bias):
    rows, d = tok.shape
    both = 2 * rows
    vm = pltpu.VMEM
    hidden = LANES * widths[2]
    small = (8, 2 * widths[1] + widths[2])
    mats = [(d, LANES * w) for w in widths]
    shape = jax.ShapeDtypeStruct
    out = [shape(m, BF) for m in mats] + [
        shape((rows, d), BF), shape((both, d), BF), shape((both, LANES * widths[0]), BF), shape((both, LANES * widths[1]), BF), shape((both, 128), F32),
        shape((rows, d), F32), shape((rows, d), F32), shape((both, d), BF), shape((both, hidden), BF), shape((both, hidden), BF),
        shape((rows, d), F32), shape((rows, d), BF), shape((rows, d), BF), shape((LANES,) + small, F32)]
    scratch = [vm(m, BF) for m in mats] + [
        vm((2, rows, d), BF), vm((2, 2, rows, d), BF), vm((rows, d), BF), vm((both, d), BF), vm((both, LANES * widths[0]), BF),
        vm((both, LANES * widths[1]), BF), vm((both, 128), F32), vm((rows, d), F32), vm((2, rows, d), BF), vm((2, rows, d), BF),
        vm((rows, d), F32), vm((both, d), BF), vm((both, hidden), BF), vm((both, hidden), BF), vm((2, rows, d), BF),
        vm((LANES,) + small, F32), vm((d // 8, sum(widths)), BF), vm((d // 8, sum(widths)), BF), vm(small, F32), vm((16, d), F32),
        pltpu.SemaphoreType.DMA((FWD_SEMS,))]
    return pl.pallas_call(
        partial(forward_kernel, widths),
        in_specs=[SMEM, SMEM] + [IN_VMEM] * 10 + [ANY, ANY],
        out_specs=[ANY] * len(out),
        out_shape=out,
        scratch_shapes=scratch,
        compiler_params=pltpu.CompilerParams(collective_id=1, has_side_effects=True, vmem_limit_bytes=67043328),
        name="forward",
    )(lengths, deal, w_qkv, w_o, w_1, w_2, b_qv, b_1, b_o, b_2, ln_gain, ln_bias, tok, cot)


def norm_back_rows(x, grad, gain):
    mag = jnp.abs(x)
    top = jnp.max(mag, axis=-1, keepdims=True)
    inv = 1.0 / (top + NORM_EPS)
    u = x * inv
    c = u - jnp.mean(u, axis=-1, keepdims=True)
    r = lax.rsqrt(jnp.mean(c * c, axis=-1, keepdims=True) + NORM_EPS)
    xhat = c * r
    t = grad * gain
    gx = grad * xhat
    along = jnp.mean(t * xhat, axis=-1, keepdims=True)
    du = r * (t - jnp.mean(t, axis=-1, keepdims=True) - xhat * along)
    at_top = mag == top
    ties = jnp.sum(jnp.where(at_top, 1.0, 0.0), axis=-1, keepdims=True)
    pull = x.shape[-1] * NORM_EPS * along * r * r * inv / ties
    side = jnp.where(x > 0, -pull, jnp.where(x < 0, pull, 0.0))
    return du * inv + jnp.where(at_top, side, 0.0), gx


BWD_SEMS = 420


def dot_g(a, b):
    return lax.dot_general(a, b, (((0,), (0,)), ((), ())), preferred_element_type=F32)


def column_sums(x):
    return jnp.sum(x, axis=0, keepdims=True)


def backward_kernel(widths, lengths, deal, ln_gain, *rest):
    ins, rest = rest[:17], rest[17:]
    (wq_i, wo_i, w1_i, w2_i, h_i, xin_i, qkv_i, heads_i, lse_i, attn_i, first_i, xmid_i, act_i, dg_i, ffn_i, res_i, grd_i) = ins
    outs, rest = rest[:9], rest[9:]
    (qkv_o, wo_o, w1_o, w2_o, out_o, ig_o, vec_o, home_o, _) = outs
    (wq, wo, w1, w2, part, grd, act, dg, xmid, first, attn, heads, qkv, lse, dfull, res, dqkv, dkv, sbuf, rbuf, zin,
     fl3, fl2, fl1, sl3, sl2, sl1, tl3, tl2, tl1, third0, third1, third2, third3, tall, wide_o, sums, sums_in, vec_all, vec, room, free, sem_ref) = rest
    xin, h = dfull, res
    mats = (dg, wo, w1, w2)
    thirds = (third0, third1, third2, third3)
    n_g = len(widths)
    sems = Sems(sem_ref)
    dp, lane = lax.axis_index("dp"), lax.axis_index("tensor")
    n_dp = 8
    core, chip = dp % 2, dp // 2
    rows, d = grd.shape
    quarter = d // 4
    per = 2 * (d // n_dp)
    wd = d // n_dp
    mate = (dp ^ 1, lane)
    cut = rows // DEAL_CUTS
    ends = []

    def local(src, dst):
        return pltpu.make_async_copy(src, dst, sem_ref.at[sems.take()])

    def remote(src, dst, device):
        a, b = sems.take(), sems.take()
        c = send(src, dst, sem_ref.at[a], sem_ref.at[b], device)
        ends.append(c)
        return c

    loads = {}
    for name, src, dst in (("ffn", ffn_i, part), ("grd", grd_i, grd), ("res", res_i, res), ("w2", w2_i, w2), ("dg", dg_i, dg), ("act", act_i, act),
                           ("w1", w1_i, w1), ("xmid", xmid_i, xmid), ("first", first_i, first), ("attn", attn_i, attn), ("wo", wo_i, wo),
                           ("heads", heads_i, heads), ("qkv", qkv_i, qkv), ("lse", lse_i, lse), ("wq", wq_i, wq), ("xin", xin_i, xin), ("h", h_i, h)):
        loads[name] = local(src, dst)
        if name not in ("xin", "h"):
            loads[name].start()
    barrier, count = greet(dp, lane, n_dp)
    held = Pack(lengths, deal, dp, lane, rows)
    relative(vec, chip, (ln_gain,))
    pl.semaphore_wait(barrier, count)
    gains = lambda i: vec[i:i + 1, :]
    sums[...] = jnp.zeros_like(sums)
    pack = lane // 2
    is_near = lane == pack + 1
    is_far = lane == 3 * pack
    block = rows // n_dp

    class Back:
        def __init__(self, i, src, same, other, out):
            self.i, self.src, self.same, self.other = i, src, same, other
            self.out = out
            z0, z1, m0, o0, h0 = [sems.take(DEAL_CUTS) for _ in range(5)]
            a0, a1 = sems.take(n_dp), sems.take(n_dp)
            self.a0, self.a1 = a0, a1
            spot = chip * 2 + pack
            kappa = core
            self.up_, self.keep_, self.give_ = [], [], []
            for n in range(DEAL_CUTS):
                rs = slice(n * cut, (n + 1) * cut)
                self.up_.append(send(src.at[rs], zin.at[i, rs], sem_ref.at[z0 + n], sem_ref.at[z1 + n], (dp, pack + 1)))
                self.keep_.append(send(same.at[rs], home_o.at[i, rs], sem_ref.at[m0 + n], sem_ref.at[h0 + n], (spot, kappa + 2 * pack)))
                self.give_.append(send(other.at[rs], home_o.at[i, rs], sem_ref.at[o0 + n], sem_ref.at[h0 + n], (spot, kappa + 2 * (1 - pack))))
            here = pl.ds(pl.multiple_of(dp * block, block), block)
            self.go_, self.stay_, self.got_ = [], [], []
            for a in range(n_dp):
                src_rows = home_o.at[i, a * block:(a + 1) * block]
                self.go_.append(send(src_rows, out.at[here], sem_ref.at[a0 + a], sem_ref.at[a1 + dp], (a, lane)))
                self.stay_.append(pltpu.make_async_copy(src_rows, out.at[here], sem_ref.at[a0 + a]))
                self.got_.append(send(src_rows, out.at[a * block:(a + 1) * block], sem_ref.at[a0 + a], sem_ref.at[a1 + a], (a, lane)))

        def start(self, n):
            pl.when(is_far)(lambda: self.up_[n].start())

        def merge(self, n):
            rs = slice(n * cut, (n + 1) * cut)

            def work():
                self.up_[n].wait_recv()
                on = held.slots(n * cut, cut, 0) >= held.cut
                mine, theirs = self.src[rs, :].astype(F32), zin[self.i, rs].astype(F32)
                self.same[rs, :] = jnp.where(on, theirs, mine).astype(BF)
                self.other[rs, :] = jnp.where(on, mine, theirs).astype(BF)
                self.keep_[n].start()
                self.give_[n].start()

            pl.when(is_near)(work)

        def home(self, n):
            self.keep_[n].wait_recv()
            for a in range(n * cut // block, (n + 1) * cut // block):
                pl.when(dp != a)(lambda: self.go_[a].start())
                pl.when(dp == a)(lambda: self.stay_[a].start())

        def sent(self):
            for n in range(DEAL_CUTS):
                pl.when(is_far)(lambda: self.up_[n].wait_send())

                def both(n=n):
                    self.keep_[n].wait_send()
                    self.give_[n].wait_send()

                pl.when(is_near)(both)

        def finish(self):
            for a in range(n_dp):
                pl.when(dp == a)(lambda: self.stay_[a].wait())

                def other(a=a):
                    self.go_[a].wait_send()
                    self.got_[a].wait_recv()

                pl.when(dp != a)(other)

    res_back = Back(0, res, dqkv.at[0:rows, 0:d], dqkv.at[rows:2 * rows, 0:d], out_o)
    grad_back = Back(1, h, act.at[0:rows, 0:d], act.at[rows:2 * rows, 0:d], ig_o)

    fls, sls, tls = (None, fl1, fl2, fl3), (None, sl1, sl2, sl3), (tl3, tl1, tl2, tl3)

    def first_place(g, i, k):
        w = widths[g]
        if g:
            return fls[g].at[i, :, k * w:(k + 1) * w]
        at = per * (2 * i + k // 2)
        return act.at[at:at + per, d + (k % 2) * w:d + (k % 2 + 1) * w]

    def second_place(g, k):
        w = widths[g]
        return sls[g].at[:, k * w:(k + 1) * w] if g else xmid.at[per * k:per * (k + 1), d // 2:d // 2 + w]

    def area(g, q, k):
        w = widths[g]
        return mats[g].at[per * q:per * (q + 1), k * w:(k + 1) * w]

    def first_pair(g, k):
        side = 1 if k < 2 else 2
        return [remote(area(g, q, k), first_place(g, i, k), (dp ^ (2 * side), lane)) for i, q in enumerate((3, side))]

    firsts = [[first_pair(g, k) for k in range(LANES)] for g in range(n_g)]
    seconds = [[remote(area(g, 2 if k < 2 else 1, k), second_place(g, k), (dp ^ (4 if k < 2 else 2), lane)) for k in range(LANES)]
               for g in range(n_g)]
    turns = [[None] + [remote(area(g, 0, k), tls[g].at[k - 1, :, 0:widths[g]], (dp, lax.rem(lane + LANES - k, LANES))) for k in range(1, LANES)]
             for g in range(n_g)]
    lasts = [remote(thirds[g].at[0], thirds[g].at[1], mate) for g in range(n_g)]

    def pass_on(g, k):
        firsts[g][k][0].wait_recv()
        here = area(g, 2 if k < 2 else 1, k)
        here[...] = (here[...].astype(F32) + first_place(g, 0, k)[...].astype(F32)).astype(BF)
        seconds[g][k].start()

    def settle(g, k):
        firsts[g][k][1].wait_recv()
        seconds[g][k].wait_recv()
        here = area(g, 0, k)
        here[...] = (here[...].astype(F32) + first_place(g, 1, k)[...].astype(F32) + second_place(g, k)[...].astype(F32)).astype(BF)
        if k:
            turns[g][k].start()

    out_copies = []

    def put(src, dst):
        c = local(src, dst)
        c.start()
        out_copies.append(c)

    mine = pl.ds(pl.multiple_of(core * wd, wd), wd)
    theirs = pl.ds(pl.multiple_of((1 - core) * wd, wd), wd)

    def lay(g, half, value):
        w = widths[g]
        if g == 3:
            tall[pl.ds(pl.multiple_of(half * w, w), w), :] = jnp.transpose(value)
        elif g == 1:
            wide_o[pl.ds(pl.multiple_of(half * w, w), w), :] = jnp.transpose(value)
        elif g == 2:
            attn[0:wd, pl.ds(pl.multiple_of(half * w, w), w)] = value
        else:
            for t in range(3):
                attn[wd * (t + 1):wd * (t + 2), pl.ds(pl.multiple_of(half * (w // 3), w // 3), w // 3)] = value[:, t * (w // 3):(t + 1) * (w // 3)]

    def total(g):
        w = widths[g]
        for k in range(1, LANES):
            turns[g][k].wait_recv()

        def add(rs):
            v = mats[g][rs, 0:w].astype(F32)
            for k in range(LANES - 1):
                v = v + tls[g][k, rs, 0:w].astype(F32)
            return v

        thirds[g][0] = add(theirs).astype(BF)
        lasts[g].start()
        lay(g, core, add(mine))

    def close(g):
        lasts[g].wait_recv()
        lay(g, 1 - core, thirds[g][1].astype(F32))
        if g == 3:
            put(tall, w2_o)
        elif g == 1:
            put(wide_o, wo_o)
        elif g == 2:
            put(attn.at[0:wd, 0:2 * widths[2]], w1_o)
        else:
            for t in range(3):
                put(attn.at[wd * (t + 1):wd * (t + 2), 0:2 * widths[1]], qkv_o.at[t])

    def blocks(g, a, b, q):
        w = widths[g]

        def one(k, carry):
            cols = pl.ds(pl.multiple_of(k * w, w), w)
            mats[g][per * q:per * (q + 1), cols] = dot_g(a[:, per * q:per * (q + 1)], b[:, cols]).astype(BF)
            return carry

        lax.fori_loop(0, LANES, one, 0)

    def grads(g, a, b, between=None):
        for q in (3, 1, 2, 0):
            blocks(g, a, b, q)
            if between:
                between(q)
            if q:
                for k in range(LANES):
                    if q == 3:
                        firsts[g][k][0].start()
                    elif (q == 1) == (k < 2):
                        firsts[g][k][1].start()

    def join(x, size, n):
        c = remote(x.at[n * size:(n + 1) * size, 0:d], x.at[rows + n * size:rows + (n + 1) * size, 0:d], mate)
        c.start()
        ends.pop()
        return c

    def fold(which, term, before=()):
        copies = []
        size = rows // 2
        for n in range(2):
            if before:
                before[n].wait_send()
            sbuf[n * size:(n + 1) * size] = term(slice(rows + n * size, rows + (n + 1) * size)).astype(BF)
            c = remote(sbuf.at[n * size:(n + 1) * size], rbuf.at[which, n * size:(n + 1) * size], mate)
            c.start()
            copies.append(c)
            if not before:
                ends.pop()
        for n in range(2):
            rs = slice(n * size, (n + 1) * size)
            part[rs, :] = term(rs)
        return copies

    loads["res"].wait()
    for n in range(DEAL_CUTS):
        res_back.start(n)
    loads["ffn"].wait()
    loads["grd"].wait()
    half = rows // 2
    joins = []

    def chunk(n, m):
        return pl.ds(pl.multiple_of(n * half + m * cut, cut), cut)

    for n in range(2):

        def norm_3(m, carry, n=n):
            rs = chunk(n, m)
            g = grd[rs, :].astype(F32)
            dx, gx = norm_back_rows(part[rs, :], g, gains(3))
            low = dx.astype(BF)
            dfull[rs, :] = low
            sums[3:4, :] += column_sums(gx)
            sums[7:8, :] += column_sums(g)
            sums[9:10, :] += column_sums(low.astype(F32))
            return carry

        lax.fori_loop(0, half // cut, norm_3, 0)
        joins.append(join(dfull, half, n))
    loads["w2"].wait()
    loads["dg"].wait()
    for c in joins:
        c.wait_recv()
    w = widths[2]
    for k in range(LANES):
        cols = slice(k * w, (k + 1) * w)

        def hidden_units(r, carry, cols=cols, k=k):
            rs = pl.ds(pl.multiple_of(r * QB, QB), QB)
            low = (jnp.dot(dfull[rs, :], w2[:, cols], preferred_element_type=F32) * dg[rs, cols].astype(F32)).astype(BF)
            dg[rs, cols] = low
            sums[16 + k:17 + k, 0:w] += column_sums(low.astype(F32))
            return carry

        lax.fori_loop(0, 2 * rows // QB, hidden_units, 0)
    loads["act"].wait()
    res_back.merge(0)
    res_back.merge(1)

    def rows_back(q):
        if q == 3:
            res_back.merge(2)
        elif q == 1:
            res_back.merge(3)
        elif q == 2:
            res_back.home(0)
            res_back.home(1)

    grads(3, dfull, act, rows_back)
    for c in joins:
        c.wait_send()
    loads["xin"].start()
    res_back.sent()
    loads["h"].start()
    loads["w1"].wait()
    copies = fold(0, lambda rs: dot_t(dg[rs, :], w1[...]))
    res_back.home(2)
    res_back.home(3)
    for k in range(LANES):
        pass_on(3, k)
    loads["xmid"].wait()
    grads(2, xmid, dg)
    for side in (2, 4):
        pl.semaphore_signal(room, inc=1, device_id=(dp ^ side, lane), device_id_type=MESH)
    loads["first"].wait()
    loads["attn"].wait()
    joins = []
    for n in range(2):
        copies[n].wait_recv()

        def middle(m, carry, n=n):
            rs = chunk(n, m)
            g = part[rs, :] + rbuf[0, rs].astype(F32)
            dx, gx = norm_back_rows(first[rs, :], g, gains(2))
            sums[2:3, :] += column_sums(gx)
            sums[6:7, :] += column_sums(g)
            f = grd[rs, :].astype(F32) + dx
            first[rs, :] = f
            dx, gx = norm_back_rows(attn[rs, :], f, gains(1))
            sums[1:2, :] += column_sums(gx)
            sums[5:6, :] += column_sums(f)
            low = dx.astype(BF)
            dqkv[rs, 0:d] = low
            sums[8:9, :] += column_sums(low.astype(F32))
            return carry

        lax.fori_loop(0, half // cut, middle, 0)
        joins.append(join(dqkv, half, n))
    loads["wo"].wait()
    loads["heads"].wait()
    for c in joins:
        c.wait_recv()
    width = heads.shape[1]

    def to_heads(r, carry):
        rs = pl.ds(pl.multiple_of(r * QB, QB), QB)
        xmid[rs, 0:width] = jnp.dot(dqkv[rs, 0:d], wo[...], preferred_element_type=F32).astype(BF)
        return carry

    lax.fori_loop(0, 2 * rows // QB, to_heads, 0)
    grads(1, dqkv, heads)
    for c in joins:
        c.wait_send()
    loads["qkv"].wait()
    loads["lse"].wait()
    def settle_all(g):
        for k in (1, 2, 3, 0):
            settle(g, k)

    def pass_all(g):
        for k in range(LANES):
            pass_on(g, k)

    def group_3():
        total(3)
        for k in range(1, LANES):
            pl.semaphore_signal(free, inc=1, device_id=(dp, lax.rem(lane + k, LANES)), device_id_type=MESH)

    events = [[lambda: settle_all(3)], [lambda: pass_all(2)], [group_3, lambda: pass_all(1)], []]
    loads["xin"].wait()
    loads["wq"].wait()
    proj = widths[0]
    kpos = held.places(0, 2 * rows, 1)
    for pair in range(width // PAIR):
        dkv[...] = jnp.zeros_like(dkv)

        def attend(i, carry, pair=pair):
            attn_back(i, pair, held, kpos, lse, xmid, qkv, dqkv, dkv)
            return carry

        lax.fori_loop(0, 2 * rows // QB, attend, 0)
        at = 3 * pair * PAIR
        dqkv[:, at + PAIR:at + 2 * PAIR] = dkv[0].astype(BF)
        dqkv[:, at + 2 * PAIR:at + 3 * PAIR] = dkv[1].astype(BF)
        if pair == 0:
            pl.semaphore_wait(room, 2)
        cols = slice(pair * proj, (pair + 1) * proj)
        for q in (3, 1 if pair < 2 else 2, 2 if pair < 2 else 1, 0):
            dg[per * q:per * (q + 1), cols] = dot_g(dfull[:, per * q:per * (q + 1)], dqkv[:, cols]).astype(BF)
            if q == 3:
                firsts[0][pair][0].start()
            elif (q == 1) == (pair < 2) and q:
                firsts[0][pair][1].start()
        for e in events[pair]:
            e()
    copies = fold(1, lambda rs: dot_t(dqkv[rs, :], wq[...]), copies)
    sums[10:12, :] += jnp.concatenate([column_sums(dqkv[:, 0:d].astype(F32)),
                                       jnp.concatenate([column_sums(dqkv[:, d:3 * d // 2].astype(F32)), jnp.zeros((1, d // 2), F32)], axis=1)], axis=0)
    loads["h"].wait()
    for n in range(2):
        copies[n].wait_recv()

        def start_rows(m, carry, n=n):
            rs = chunk(n, m)
            g = part[rs, :] + rbuf[1, rs].astype(F32)
            dx, gx = norm_back_rows(h[rs, :].astype(F32), g, gains(0))
            sums[0:1, :] += column_sums(gx)
            sums[4:5, :] += column_sums(g)
            f = first[rs, :] + dx
            for q in range(4):
                cols = pl.ds(pl.multiple_of((chip ^ q) * quarter, quarter), quarter)
                h[rs, cols] = f[:, q * quarter:(q + 1) * quarter].astype(BF)
            return carry

        lax.fori_loop(0, half // cut, start_rows, 0)
        for m in range(half // cut):
            grad_back.start(n * (half // cut) + m)
    vec_all[...] = jnp.zeros_like(vec_all)
    for q in range(4):
        cols = pl.ds(pl.multiple_of((chip ^ q) * quarter, quarter), quarter)
        vec_all[0:10, cols] = sums[0:10, q * quarter:(q + 1) * quarter]
    hw = widths[1]
    for k in range(LANES):
        owner = lax.rem(lane + LANES - k, LANES)
        cols = pl.ds(pl.multiple_of(owner * 2 * hw + core * hw, hw), hw)
        for row, t in ((10, 0), (11, 2)):
            at = (3 * k + t) * hw
            vec_all[row:row + 1, cols] = sums[10 + at // d:11 + at // d, at % d:at % d + hw]
        vec_all[pl.ds(12 + owner, 1), pl.ds(pl.multiple_of(core * w, w), w)] = sums[16 + k:17 + k, 0:w]
    partners = [mate, (dp ^ 2, lane), (dp ^ 4, lane), (dp, lane ^ 1), (dp, lane ^ 2)]
    rounds = [remote(vec_all, sums_in.at[i], partners[i]) for i in range(5)]

    def vec_round(i):
        rounds[i].wait()
        vec_all[...] = vec_all[...] + sums_in[i]
        if i < 4:
            rounds[i + 1].start()

    rounds[0].start()
    settle_all(2)
    vec_round(0)
    grad_back.merge(0)
    settle_all(1)
    close(3)
    vec_round(1)
    grad_back.merge(1)
    pass_on(0, 0)
    pass_on(0, 1)
    grad_back.merge(2)
    grad_back.home(0)
    vec_round(2)
    pass_on(0, 2)
    pass_on(0, 3)
    grad_back.merge(3)
    grad_back.home(1)
    vec_round(3)
    total(2)
    grad_back.home(2)
    total(1)
    grad_back.home(3)
    pl.semaphore_wait(free, LANES - 1)
    settle_all(0)
    vec_round(4)
    vec_o[...] = vec_all[...]
    close(2)
    close(1)
    total(0)
    close(0)
    res_back.finish()
    grad_back.sent()
    grad_back.finish()
    for c in out_copies:
        c.wait()
    for c in ends:
        if not any(c is r for r in rounds):
            c.wait_send()


def attn_back(i, pair, held, kpos, lse, grads, qkv, dqkv, dkv):
    begin = pl.multiple_of(i * QB, QB)
    rs = pl.ds(begin, QB)
    bias = held.bias(begin, kpos)
    lane = lax.broadcasted_iota(jnp.int32, (1, PAIR), 1)
    at = 3 * pair * PAIR
    query = qkv[rs, at:at + PAIR]
    key, value = qkv[:, at + PAIR:at + 2 * PAIR], qkv[:, at + 2 * PAIR:at + 3 * PAIR]
    grad = grads[rs, pair * PAIR:(pair + 1) * PAIR]
    dq = jnp.zeros(query.shape, F32)
    dk = jnp.zeros(key.shape, F32)
    dv = jnp.zeros(key.shape, F32)
    for side in range(2):
        mine = (lane >= side * DH) & (lane < (side + 1) * DH)
        piece = jnp.where(mine, query * 0.125, 0.0).astype(BF)
        gpart = jnp.where(mine, grad, jnp.zeros_like(grad))
        score = dot_t(piece, key) + bias
        index = pair * 2 + side
        prob = jnp.exp(score - lse[rs, index:index + 1])
        gprob = dot_t(gpart, value)
        inner = jnp.sum(prob * gprob, axis=-1, keepdims=True)
        gscore = (prob * (gprob - inner)).astype(BF)
        dq += jnp.dot(gscore, jnp.where(mine, key, jnp.zeros_like(key)), preferred_element_type=F32)
        dk += dot_g(gscore, piece)
        dv += dot_g(prob.astype(BF), gpart)
    dqkv[rs, at:at + PAIR] = (dq * 0.125).astype(BF)
    dkv[0] += dk
    dkv[1] += dv


def backward_call(widths, lengths, deal, ln_gain, saved):
    (wq, wo, w1, w2, h, xin, qkv, heads, lse, attn, first, xmid, act, dg, ffn, res, grd) = saved
    rows, d = h.shape
    per, wd = d // 4, d // 8
    shape, vm = jax.ShapeDtypeStruct, pltpu.VMEM
    like = lambda x: vm(x.shape, x.dtype)
    out = [shape((3, wd, 2 * widths[1]), F32), shape((2 * widths[1], wd), F32), shape((wd, 2 * widths[2]), F32), shape((2 * widths[3], wd), F32),
           shape((rows, d), BF), shape((rows, d), BF), shape((16, d), F32), shape((2, rows, d), BF), shape((8, 128), F32)]
    scratch = [like(x) for x in (wq, wo, w1, w2, ffn, grd, act, dg, xmid, first, attn, heads, qkv, lse, xin, h)]
    scratch += [vm(qkv.shape, BF), vm((2, 2 * rows, PAIR), F32), vm((rows, d), BF), vm((2, rows, d), BF), vm((2, rows, d), BF)]
    order = (3, 2, 1)
    scratch += [vm((2, per, LANES * widths[g]), BF) for g in order]
    scratch += [vm((per, LANES * widths[g]), BF) for g in order]
    scratch += [vm((LANES - 1, per, widths[g]), BF) for g in order]
    scratch += [vm((2, wd, w), BF) for w in widths]
    scratch += [vm((2 * widths[3], wd), F32), vm((2 * widths[1], wd), F32), vm((24, d), F32), vm((5, 16, d), F32), vm((16, d), F32), vm((8, d), F32),
                pltpu.SemaphoreType.REGULAR, pltpu.SemaphoreType.REGULAR, pltpu.SemaphoreType.DMA((BWD_SEMS,))]
    return pl.pallas_call(
        partial(backward_kernel, widths),
        in_specs=[SMEM, SMEM, IN_VMEM] + [ANY] * 17,
        out_specs=[ANY] * 6 + [IN_VMEM, ANY, IN_VMEM],
        out_shape=out,
        scratch_shapes=scratch,
        compiler_params=pltpu.CompilerParams(collective_id=2, has_side_effects=True, vmem_limit_bytes=67043328),
        name="backward",
    )(lengths, deal, ln_gain, *saved)


def feature_turn(x):
    n = lax.axis_size("dp") // 2
    chip = lax.axis_index("dp") // 2
    lead = x.shape[:-1]
    width = x.shape[-1] // n
    bits = n.bit_length() - 1
    y = x.reshape(lead + (2,) * bits + (width,))
    for b in range(bits):
        axis = len(lead) + bits - 1 - b
        y = jnp.where((chip >> b) & 1 == 1, jnp.flip(y, axis), y)
    return y.reshape(x.shape)


def body(tokens, cotangent, lengths, deal, w_qkv, w_o, w_1, w_2, b_qv, b_o, b_1, b_2, ln_gain, ln_bias):
    n_dp, lanes = lax.axis_size("dp"), lax.axis_size("tensor")
    dp, lane = lax.axis_index("dp"), lax.axis_index("tensor")
    core, chip = dp % 2, dp // 2
    rows = tokens.shape[0]
    both = ("dp", "tensor")
    near, far = deal_perms(n_dp)
    back_near, back_far = [(b, a) for a, b in near], [(b, a) for a, b in far]

    if n_dp == 8 and lanes == LANES:
        hw, fw = w_o.shape[0] // 2, w_1.shape[1] // 2
        widths = (3 * hw, hw, fw, fw)
        saved = forward_call(widths, tokens, cotangent, lengths, deal, w_qkv, w_o, w_1, w_2, b_qv, b_1[None], b_o[None], b_2[None], ln_gain, ln_bias)
        qkv_grad, out_grad, up_grad, down_grad, output, input_grad, vector, _, _ = backward_call(widths, lengths, deal, ln_gain, saved[:17])
        mine = lambda x: lax.dynamic_slice_in_dim(x.reshape(-1, lanes, x.shape[-1] // lanes), lane, 1, 1)[:, 0]
        bias_1_total = lax.dynamic_slice_in_dim(vector, 12 + lane, 1, 0)[0]
        return (output, input_grad, qkv_grad, out_grad, up_grad, down_grad, mine(vector[10:12]), vector[8], bias_1_total, vector[9],
                vector[0:4], vector[4:8])

    per = lengths.shape[0] // n_dp

    def pack_ends(pack):
        picked = lax.dynamic_slice_in_dim(deal, pack * per, per)
        lookup = picked[:, None] == jnp.arange(lengths.shape[0], dtype=jnp.int32)[None, :]
        lens = jnp.sum(jnp.where(lookup, lengths[None, :], 0), axis=1)
        ends = jnp.sum(jnp.where(jnp.arange(per)[:, None] >= jnp.arange(per)[None, :], lens[None, :], 0), axis=1)
        return ends, ends - lens, jnp.sum(jnp.where(lens == HALF, ends - lens, 0))

    half = lane % 2
    ends, starts, cut = pack_ends(chip * 2 + lane // 2)
    _, _, cut_home = pack_ends(dp)
    index = jnp.arange(rows, dtype=jnp.int32)
    slots = jnp.concatenate([core * rows + index, (1 - core) * rows + index])
    place = jnp.where(slots >= cut, slots + HALF * half, slots + HALF * (1 - half))
    seg_start = jnp.max(jnp.where(place[:, None] >= starts[None, :], starts[None, :], 0), axis=1)
    qpos, qstart, kpos = place[:, None], seg_start[:, None], place[None, :]
    keep = ((core * rows + index) >= cut)[:, None]
    keep_home = (((lane % 2) * rows + index) >= cut_home)[:, None]

    def deal_in(x):
        moved = lax.all_to_all(x, "dp", split_axis=0, concat_axis=0, tiled=True)
        return jnp.where(keep, lax.ppermute(moved, both, near), lax.ppermute(moved, both, far))

    def deal_out(x):
        moved = jnp.where(keep_home, lax.ppermute(x, both, back_near), lax.ppermute(x, both, back_far))
        return lax.all_to_all(moved, "dp", split_axis=0, concat_axis=0, tiled=True)

    def halves(x):
        w = x.shape[-1] // 2
        return (lax.dynamic_slice_in_dim(x, core * w, w, x.ndim - 1), lax.dynamic_slice_in_dim(x, (1 - core) * w, w, x.ndim - 1))

    qm, qo = halves(w_qkv)
    om, oo = halves(w_o.T)
    um, uo = halves(w_1)
    dm, do = halves(w_2.T)
    own = jnp.concatenate([qm[0], qm[1], qm[2], om, um, dm], axis=1)
    other = jnp.concatenate([qo[0], qo[1], qo[2], oo, uo, do], axis=1)
    hw, fw = om.shape[1], um.shape[1]
    widths = (3 * hw, hw, fw, fw)
    small = jnp.concatenate([halves(b_qv[0:1])[0], halves(b_qv[1:2])[0], halves(b_1[None])[0]], axis=1)
    small = jnp.concatenate([small, jnp.zeros((7, small.shape[1]), F32)])
    order = (lane - jnp.arange(lanes)) % lanes
    gain, shift = feature_turn(ln_gain), feature_turn(ln_bias)
    bias_o, bias_2 = feature_turn(b_o[None])[0], feature_turn(b_2[None])[0]

    def join(x):
        return jnp.concatenate([x, swap_dp(x, 1)], axis=0)

    def fold(x):
        return x[:rows] + swap_dp(x[rows:].astype(BF), 1).astype(F32)

    mm = partial(jnp.dot, preferred_element_type=F32)
    mm_t = lambda a, b: lax.dot_general(a, b, (((1,), (1,)), ((), ())), preferred_element_type=F32)
    mm_g = lambda a, b: lax.dot_general(a, b, (((0,), (0,)), ((), ())), preferred_element_type=F32)
    if True:
        blocks = gather_weights(own, other)
        wq, wo, w1, w2 = (weight_of(blocks, sum(widths[:i]), w) for i, w in enumerate(widths))
        smalls = jnp.take(lax.all_gather(small[0], "tensor"), order, axis=0)
        bias_q, bias_v, bias_1 = smalls[:, :hw], smalls[:, hw:2 * hw], smalls[:, 2 * hw:].reshape(-1)
        bias_qkv = jnp.concatenate([bias_q, jnp.zeros_like(bias_q), bias_v], axis=1).reshape(-1)
        hidden = feature_turn(deal_in(tokens)).astype(F32)
        normed_in = join(scaled_norm(hidden, gain[0], shift[0]).astype(BF))
        qkv = (mm(normed_in, wq) + bias_qkv).astype(BF)
        heads_out, lse = attn_forward(qpos, qstart, kpos, qkv)
        attn_out = fold(mm_t(heads_out, wo)) + bias_o
        first_sum = hidden + scaled_norm(attn_out, gain[1], shift[1])
        normed_mid = join(scaled_norm(first_sum, gain[2], shift[2]).astype(BF))
        pre_act = mm(normed_mid, w1) + bias_1
        cdf = 0.5 + 0.5 * lax.erf(pre_act * 0.7071067811865476)
        act = (pre_act * cdf).astype(BF)
        dgelu = (cdf + pre_act * (0.3989422804014327 * jnp.exp(-0.5 * pre_act * pre_act))).astype(BF)
        ffn_out = fold(mm_t(act, w2)) + bias_2
        result = feature_turn((first_sum + scaled_norm(ffn_out, gain[3], shift[3])).astype(BF))
        grad_result = feature_turn(deal_in(cotangent)).astype(F32)

    grad_ffn, gain_3, shift_3 = norm_back(ffn_out, gain[3], shift[3], grad_result)
    grad_ffn_low = grad_ffn.astype(BF)
    bias_2_grad = jnp.sum(grad_ffn_low.astype(F32), axis=0)
    grad_ffn_full = join(grad_ffn_low)
    grad_act = mm(grad_ffn_full, w2)
    down_part = mm_g(grad_ffn_full, act).astype(BF)
    grad_pre = (grad_act * dgelu.astype(F32)).astype(BF)
    bias_1_grad = jnp.sum(grad_pre.astype(F32), axis=0)
    grad_mid = fold(mm_t(grad_pre, w1))
    up_part = mm_g(normed_mid, grad_pre).astype(BF)
    grad_first_part, gain_2, shift_2 = norm_back(first_sum, gain[2], shift[2], grad_mid)
    grad_first = grad_result + grad_first_part
    grad_attn, gain_1, shift_1 = norm_back(attn_out, gain[1], shift[1], grad_first)
    grad_attn_low = grad_attn.astype(BF)
    bias_o_grad = jnp.sum(grad_attn_low.astype(F32), axis=0)
    grad_attn_full = join(grad_attn_low)
    grad_heads = mm(grad_attn_full, wo).astype(BF)
    out_part = mm_g(grad_attn_full, heads_out).astype(BF)
    grad_qkv = attn_backward(qpos, qstart, kpos, lse, grad_heads, qkv)
    bias_qkv_grad = jnp.sum(grad_qkv.astype(F32), axis=0).reshape(lanes, 3, hw)
    grad_in = fold(mm_t(grad_qkv, wq))
    qkv_part = mm_g(normed_in, grad_qkv).astype(BF)
    grad_hidden_part, gain_0, shift_0 = norm_back(hidden, gain[0], shift[0], grad_in)
    grad_hidden = feature_turn((grad_first + grad_hidden_part).astype(BF))

    def by_lane(x):
        x = jnp.take(x.reshape(lanes, -1), order, axis=0)
        both_halves = jnp.stack([jnp.where(core == 0, x, 0.0), jnp.where(core == 1, x, 0.0)], axis=1)
        return both_halves.reshape(-1)

    d = tokens.shape[1]
    stack = jnp.stack([gain_0, gain_1, gain_2, gain_3, shift_0, shift_1, shift_2, shift_3, bias_o_grad, bias_2_grad])
    vector = jnp.concatenate([feature_turn(stack).reshape(-1), by_lane(bias_qkv_grad[:, 0]), by_lane(bias_qkv_grad[:, 2]), by_lane(bias_1_grad)])
    parts = [qkv_part, out_part, up_part, down_part]
    output, input_grad = deal_out(result), deal_out(grad_hidden)
    vector = lax.psum(vector, both)
    shards = [scatter_grads([p.astype(F32)]) for p in parts]
    gain_total, shift_total = vector[:4 * d].reshape(4, d), vector[4 * d:8 * d].reshape(4, d)
    bias_o_total, bias_2_total = vector[8 * d:9 * d], vector[9 * d:10 * d]
    mine = lambda x: lax.dynamic_slice_in_dim(x.reshape(lanes, -1), lane, 1, 0)[0]
    bias_qv_total = jnp.stack([mine(vector[10 * d:11 * d]), mine(vector[11 * d:12 * d])])
    bias_1_total = mine(vector[12 * d:])

    spread = lambda x: jnp.concatenate([x[0], x[1]], axis=-1)
    qkv_grad, out_grad, up_grad, down_grad = shards
    qkv_out = jnp.stack([spread(qkv_grad[:, :, i * hw:(i + 1) * hw]) for i in range(3)])
    return (
        output, input_grad, qkv_out, spread(out_grad).T, spread(up_grad), spread(down_grad).T,
        bias_qv_total, bias_o_total, bias_1_total, bias_2_total, gain_total, shift_total,
    )


def solution(mesh):
    rows = P(("dp", "tensor"), None)
    weights = (P(None, "dp", "tensor"), P("tensor", "dp"), P("dp", "tensor"), P("tensor", "dp"))
    vectors = (P(None, "tensor"), P(), P("tensor"), P(), P(), P())
    return jax.shard_map(
        body,
        mesh=mesh,
        in_specs=(rows, rows, P(), P()) + weights + vectors,
        out_specs=(rows, rows) + weights + vectors,
        check_vma=False,
    )
```

profile of v0, /device:TPU:1, one launch (start us, length us, event | category | flops | bytes accessed | tf_op | source)
XLA Modules:
  0.0 388.1 jit_solution(2238039514917424905)
XLA Ops:
  0.6 175.5 %forward.1 = (bf16[1024,1536]{1,0:T(8,128)(2,1)}, bf16[1024,512]{1,0:T(8,128)(2,1)}, bf16[1024,2048]{1,0:T(8,128)(2,1)}, bf16[1024,2048]{1,0:T(8,128)(2,1)}, bf1...) custom-call(s32[32]{0:T(128)} %lengths.3, ...), custom_call_target="tpu_custom_call" | custom-call | tf_op jit(solution)/shard_map/forward/pallas_call | solution.py:764
  176.2 199.7 %backward.1 = (f32[3,128,256]{2,1,0:T(8,128)}, f32[256,128]{1,0:T(8,128)}, f32[128,1024]{1,0:T(8,128)}, f32[1024,128]{1,0:T(8,128)}, bf16[512,1024]{1,0:T(8,128)...) custom-call(s32[32]{0:T(128)} %lengths.3, s32[32]{0:T(128)} %deal.3, ...), custom_call_target="tpu_custom_call" | custom-call | tf_op jit(solution)/shard_map/backward/pallas_call | solution.py:1343
  375.9 0.0 copy-start.2
  375.9 0.0 copy-start.3
  376.0 0.0 copy-start.1
  376.0 1.5 fusion
  377.4 0.8 slice.15
  378.2 0.6 copy.28
  378.8 1.5 fusion.1
  380.3 0.0 copy-start
  380.3 2.3 copy.35
  382.6 2.3 copy.36
  384.9 0.0 copy-done.2
  384.9 0.7 copy.37
  385.6 0.0 copy-done.3
  385.6 0.7 copy.38
  386.3 0.0 copy-done.1
  386.3 0.8 copy.39
  387.1 0.0 copy-done
  387.1 0.8 copy.40
  (2 shorter events, 0.0 us)
Async XLA Ops:
  375.9 8.9 %copy-start.2 = (f32[3,128,256]{2,1,0:T(8,128)S(1)}, f32[3,128,256]{2,1,0:T(8,128)}, u32[]{:S(2)}) copy-start(f32[3,128,256]{2,1,0:T(8,128)} %get-tuple-element.79) | copy-start | bytes 1179652
  375.9 9.7 %copy-start.3 = (f32[256,128]{1,0:T(8,128)S(1)}, f32[256,128]{1,0:T(8,128)}, u32[]{:S(2)}) copy-start(f32[256,128]{1,0:T(8,128)} %get-tuple-element.80) | copy-start | bytes 393220
  376.0 10.3 %copy-start.1 = (f32[128,1024]{1,0:T(8,128)S(1)}, f32[128,1024]{1,0:T(8,128)}, u32[]{:S(2)}) copy-start(f32[128,1024]{1,0:T(8,128)} %get-tuple-element.81) | copy-start | bytes 1572868
  380.3 6.8 %copy-start = (f32[1024,128]{1,0:T(8,128)S(1)}, f32[1024,128]{1,0:T(8,128)}, u32[]{:S(2)}) copy-start(f32[1024,128]{1,0:T(8,128)} %get-tuple-element.82) | copy-start | bytes 1572868
where the time goes:
time: 391 us; the launch traced here: 388 us
  Pallas kernels  375 us (96%)
  local copies, waits for them, and re-layouts  11.9 us (3%)
    pallas_call x1, Pallas kernels, backward_call(): pl.pallas_call(partial(backward_kernel, widths), in_specs=[SMEM, SMEM, IN...  200 us
    pallas_call x1, Pallas kernels, forward_call(): pl.pallas_call(partial(forward_kernel, widths), in_specs=[SMEM, SMEM] + [...  176 us
    unnamed x15, local copies, waits for them, and re-layouts  8.17 us

commit v1 on v0

--- a/solution.py
+++ b/solution.py
@@ -541,19 +541,20 @@
         for g in groups:
             plane(g, t + 1)
 
-    for g in (0, 1, 2):
+    for g in range(4):
         pair_in(g)
-        plane(g, 0)
+        if g < 3:
+            plane(g, 0)
     forward_on(early, 0)
     forward_on((2,), 0)
     forward_on(early, 1)
+    turn_in(3, 0)
     deal_on(0)
     forward_on((2,), 1)
     forward_on(early, 2)
     for k in range(LANES):
         for g in early:
             far_go(g, k)
-    pair_in(3)
     plane(3, 0)
     deal_start(1)
     joins = []
@@ -571,9 +572,11 @@
         h[rs, :] = x.astype(BF)
         xin[rs, :] = norm_rows(x, gains(0), gains(4)).astype(BF)
         join_send(xin, n, cut)
+        if n == 1:
+            forward_on((2,), 2)
         if n == 2:
-            forward_on((2,), 2)
-    forward_on((3,), 0)
+            turn_in(3, 1)
+    plane(3, 1)
     for c in smalls:
         c.wait_recv()
     all_in(0)
@@ -597,7 +600,7 @@
         lax.fori_loop(0, 2 * rows // QB, project, 0)
         far_go(2, k)
     put(qkv, qkv_o)
-    forward_on((3,), 1)
+    plane(3, 2)
 
     kpos = held.places(0, 2 * rows, 1)
 
@@ -1109,9 +1112,6 @@
             res_back.merge(2)
         elif q == 1:
             res_back.merge(3)
-        elif q == 2:
-            res_back.home(0)
-            res_back.home(1)
 
     grads(3, dfull, act, rows_back)
     for c in joins:
@@ -1121,8 +1121,6 @@
     loads["h"].start()
     loads["w1"].wait()
     copies = fold(0, lambda rs: dot_t(dg[rs, :], w1[...]))
-    res_back.home(2)
-    res_back.home(3)
     for k in range(LANES):
         pass_on(3, k)
     loads["xmid"].wait()
@@ -1183,7 +1181,7 @@
         for k in range(1, LANES):
             pl.semaphore_signal(free, inc=1, device_id=(dp, lax.rem(lane + k, LANES)), device_id_type=MESH)
 
-    events = [[lambda: settle_all(3)], [lambda: pass_all(2)], [group_3, lambda: pass_all(1)], []]
+    events = [[lambda: settle_all(3)], [lambda: pass_all(2)], [group_3, lambda: pass_all(1)], [lambda: settle_all(2)] + [lambda n=n: res_back.home(n) for n in range(DEAL_CUTS)]]
     loads["xin"].wait()
     loads["wq"].wait()
     proj = widths[0]
@@ -1254,7 +1252,6 @@
             rounds[i + 1].start()
 
     rounds[0].start()
-    settle_all(2)
     vec_round(0)
     grad_back.merge(0)
     settle_all(1)

time: 391 us -> 364 us (0.931)
  Pallas kernels: 375 us -> 349 us
    pallas_call x1, Pallas kernels: 176 us -> 162 us  [forward_call(): pl.pallas_call(partial(forward_kernel, widths), in_specs=[SMEM, SMEM] + [...]
    pallas_call x1, Pallas kernels: 200 us -> 187 us  [backward_call(): pl.pallas_call(partial(backward_kernel, widths), in_specs=[SMEM, SMEM, IN...]
where the time goes in v1:
time: 364 us; the launch traced here: 361 us
  Pallas kernels  349 us (96%)
  local copies, waits for them, and re-layouts  11.9 us (3%)
    pallas_call x1, Pallas kernels, backward_call(): pl.pallas_call(partial(backward_kernel, widths), in_specs=[SMEM, SMEM, IN...  187 us
    pallas_call x1, Pallas kernels, forward_call(): pl.pallas_call(partial(forward_kernel, widths), in_specs=[SMEM, SMEM] + [...  162 us
    unnamed x15, local copies, waits for them, and re-layouts  8.17 us

profile of v1, /device:TPU:1, one launch (start us, length us, event | category | flops | bytes accessed | tf_op | source)
XLA Modules:
  0.0 361.5 jit_solution(17182977470535834775)
XLA Ops:
  0.6 161.9 %forward.1 = (bf16[1024,1536]{1,0:T(8,128)(2,1)}, bf16[1024,512]{1,0:T(8,128)(2,1)}, bf16[1024,2048]{1,0:T(8,128)(2,1)}, bf16[1024,2048]{1,0:T(8,128)(2,1)}, bf1...) custom-call(s32[32]{0:T(128)} %lengths.3, ...), custom_call_target="tpu_custom_call" | custom-call | tf_op jit(solution)/shard_map/forward/pallas_call | solution.py:767
  162.6 186.7 %backward.1 = (f32[3,128,256]{2,1,0:T(8,128)}, f32[256,128]{1,0:T(8,128)}, f32[128,1024]{1,0:T(8,128)}, f32[1024,128]{1,0:T(8,128)}, bf16[512,1024]{1,0:T(8,128)...) custom-call(s32[32]{0:T(128)} %lengths.3, s32[32]{0:T(128)} %deal.3, ...), custom_call_target="tpu_custom_call" | custom-call | tf_op jit(solution)/shard_map/backward/pallas_call | solution.py:1340
  349.3 0.0 copy-start.2
  349.3 0.0 copy-start.3
  349.3 0.0 copy-start.1
  349.3 1.5 fusion
  350.8 0.8 slice.15
  351.6 0.6 copy.28
  352.2 1.5 fusion.1
  353.7 0.0 copy-start
  353.7 2.3 copy.35
  356.0 2.3 copy.36
  358.2 0.0 copy-done.2
  358.3 0.7 copy.37
  359.0 0.0 copy-done.3
  359.0 0.7 copy.38
  359.7 0.0 copy-done.1
  359.7 0.8 copy.39
  360.5 0.0 copy-done
  360.5 0.8 copy.40
  (2 shorter events, 0.0 us)
Async XLA Ops:
  349.3 8.9 %copy-start.2 = (f32[3,128,256]{2,1,0:T(8,128)S(1)}, f32[3,128,256]{2,1,0:T(8,128)}, u32[]{:S(2)}) copy-start(f32[3,128,256]{2,1,0:T(8,128)} %get-tuple-element.79) | copy-start | bytes 1179652
  349.3 9.7 %copy-start.3 = (f32[256,128]{1,0:T(8,128)S(1)}, f32[256,128]{1,0:T(8,128)}, u32[]{:S(2)}) copy-start(f32[256,128]{1,0:T(8,128)} %get-tuple-element.80) | copy-start | bytes 393220
  349.3 10.3 %copy-start.1 = (f32[128,1024]{1,0:T(8,128)S(1)}, f32[128,1024]{1,0:T(8,128)}, u32[]{:S(2)}) copy-start(f32[128,1024]{1,0:T(8,128)} %get-tuple-element.81) | copy-start | bytes 1572868
  353.7 6.8 %copy-start = (f32[1024,128]{1,0:T(8,128)S(1)}, f32[1024,128]{1,0:T(8,128)}, u32[]{:S(2)}) copy-start(f32[1024,128]{1,0:T(8,128)} %get-tuple-element.82) | copy-start | bytes 1572868

commit v2 on v1

--- a/solution.py
+++ b/solution.py
@@ -549,8 +549,8 @@
     forward_on((2,), 0)
     forward_on(early, 1)
     turn_in(3, 0)
+    forward_on((2,), 1)
     deal_on(0)
-    forward_on((2,), 1)
     forward_on(early, 2)
     for k in range(LANES):
         for g in early:
@@ -1181,7 +1181,7 @@
         for k in range(1, LANES):
             pl.semaphore_signal(free, inc=1, device_id=(dp, lax.rem(lane + k, LANES)), device_id_type=MESH)
 
-    events = [[lambda: settle_all(3)], [lambda: pass_all(2)], [group_3, lambda: pass_all(1)], [lambda: settle_all(2)] + [lambda n=n: res_back.home(n) for n in range(DEAL_CUTS)]]
+    events = [[lambda: settle_all(3)], [lambda: pass_all(2)], [group_3, lambda: pass_all(1)], [lambda: settle_all(2), lambda: settle_all(1)] + [lambda n=n: res_back.home(n) for n in range(DEAL_CUTS)]]
     loads["xin"].wait()
     loads["wq"].wait()
     proj = widths[0]
@@ -1254,7 +1254,6 @@
     rounds[0].start()
     vec_round(0)
     grad_back.merge(0)
-    settle_all(1)
     close(3)
     vec_round(1)
     grad_back.merge(1)
@@ -1348,6 +1347,35 @@
     )(lengths, deal, ln_gain, *saved)
 
 
+def results_kernel(vec, *refs):
+    lane = lax.axis_index("tensor")
+    count = (len(refs) - 6) // 2
+    for src, dst in zip(refs[:count], refs[count:2 * count]):
+        dst[...] = src[...]
+    qv, b_o, b_1, b_2, gain, shift = refs[2 * count:]
+    part = qv.shape[1]
+    qv[...] = vec[10:12, pl.ds(pl.multiple_of(lane * part, part), part)]
+    b_o[...] = vec[8:9, :]
+    b_1[...] = vec[pl.ds(12 + lane, 1), :]
+    b_2[...] = vec[9:10, :]
+    gain[...] = vec[0:4, :]
+    shift[...] = vec[4:8, :]
+
+
+def results_call(vec, large, part):
+    d = vec.shape[1]
+    shape = jax.ShapeDtypeStruct
+    small = [shape((2, part), F32), shape((1, d), F32), shape((1, d), F32), shape((1, d), F32), shape((4, d), F32), shape((4, d), F32)]
+    return pl.pallas_call(
+        results_kernel,
+        in_specs=[IN_VMEM] * (1 + len(large)),
+        out_specs=[IN_VMEM] * (len(large) + 6),
+        out_shape=[shape(x.shape, x.dtype) for x in large] + small,
+        compiler_params=pltpu.CompilerParams(vmem_limit_bytes=67043328),
+        name="results",
+    )(vec, *large)
+
+
 def feature_turn(x):
     n = lax.axis_size("dp") // 2
     chip = lax.axis_index("dp") // 2
@@ -1375,10 +1403,9 @@
         widths = (3 * hw, hw, fw, fw)
         saved = forward_call(widths, tokens, cotangent, lengths, deal, w_qkv, w_o, w_1, w_2, b_qv, b_1[None], b_o[None], b_2[None], ln_gain, ln_bias)
         qkv_grad, out_grad, up_grad, down_grad, output, input_grad, vector, _, _ = backward_call(widths, lengths, deal, ln_gain, saved[:17])
-        mine = lambda x: lax.dynamic_slice_in_dim(x.reshape(-1, lanes, x.shape[-1] // lanes), lane, 1, 1)[:, 0]
-        bias_1_total = lax.dynamic_slice_in_dim(vector, 12 + lane, 1, 0)[0]
-        return (output, input_grad, qkv_grad, out_grad, up_grad, down_grad, mine(vector[10:12]), vector[8], bias_1_total, vector[9],
-                vector[0:4], vector[4:8])
+        *large, qv, bias_o_sum, bias_1_sum, bias_2_sum, gain_sum, shift_sum = results_call(
+            vector, (output, input_grad, qkv_grad, out_grad, up_grad, down_grad), b_qv.shape[1])
+        return (*large, qv, bias_o_sum[0], bias_1_sum[0], bias_2_sum[0], gain_sum, shift_sum)
 
     per = lengths.shape[0] // n_dp
 

time: 364 us -> 356 us (0.978)
  local copies, waits for them, and re-layouts: 11.9 us -> 0 us
  Pallas kernels: 349 us -> 353 us
    unnamed x15 -> x0, local copies, waits for them, and re-layouts: 8.17 us -> none
    pallas_call x0 -> x1, Pallas kernels: none -> 3.97 us  [results_call(): pl.pallas_call(results_kernel, in_specs=[IN_VMEM] * (1 + len(large)), out...]
    slice x3 -> x0, local copies, waits for them, and re-layouts: 3.72 us -> none  [the longest x1 1.48 us: body(): vector[4:8]]
where the time goes in v2:
time: 356 us; the launch traced here: 354 us
  Pallas kernels  353 us (99%)
    pallas_call x1, Pallas kernels, backward_call(): pl.pallas_call(partial(backward_kernel, widths), in_specs=[SMEM, SMEM, IN...  187 us
    pallas_call x1, Pallas kernels, forward_call(): pl.pallas_call(partial(forward_kernel, widths), in_specs=[SMEM, SMEM] + [...  162 us

profile of v2, /device:TPU:1, one launch (start us, length us, event | category | flops | bytes accessed | tf_op | source)
XLA Modules:
  0.0 353.6 jit_solution(16356286629600949123)
XLA Ops:
  0.6 161.9 %forward.1 = (bf16[1024,1536]{1,0:T(8,128)(2,1)}, bf16[1024,512]{1,0:T(8,128)(2,1)}, bf16[1024,2048]{1,0:T(8,128)(2,1)}, bf16[1024,2048]{1,0:T(8,128)(2,1)}, bf1...) custom-call(s32[32]{0:T(128)} %lengths.3, ...), custom_call_target="tpu_custom_call" | custom-call | tf_op jit(solution)/shard_map/forward/pallas_call | solution.py:767
  162.6 186.7 %backward.1 = (f32[3,128,256]{2,1,0:T(8,128)}, f32[256,128]{1,0:T(8,128)}, f32[128,1024]{1,0:T(8,128)}, f32[1024,128]{1,0:T(8,128)}, bf16[512,1024]{1,0:T(8,128)...) custom-call(s32[32]{0:T(128)} %lengths.3, s32[32]{0:T(128)} %deal.3, ...), custom_call_target="tpu_custom_call" | custom-call | tf_op jit(solution)/shard_map/backward/pallas_call | solution.py:1339
  349.3 4.0 %results.1 = (bf16[512,1024]{1,0:T(8,128)(2,1)}, bf16[512,1024]{1,0:T(8,128)(2,1)}, f32[3,128,256]{2,1,0:T(8,128)}, f32[256,128]{1,0:T(8,128)}, f32[128,1024]{1,...) custom-call(f32[16,1024]{1,0:T(8,128)} %get-tuple-element.65.vec, ...), custom_call_target="tpu_custom_call" | custom-call | tf_op jit(solution)/shard_map/results/pallas_call | solution.py:1369
